TPU v7x, 32 devices: a whole 2x2x4 slice. The times are simulated.
32 devices in a mesh: cell: 8 (over z, x), desc: 4 (over y, core).
Axes of the slice: x: 2, y: 2, z: 4, core: 2. Of those that a mesh axis runs over, the one named last changes fastest.
Arguments:
- cells: float32 [8192, 256], P('cell'), may hold values from -128 to 128
- descs: float32 [8192, 256], P('desc'), may hold values from -4 to 4
- g_start: float32 [8192], P('desc'), may hold values from -8 to 8
- cot_f: float32 [8192], P('cell'), may hold values from -24 to 24
- cot_g: float32 [8192], P('desc'), may hold values from -24 to 24
Outputs:
- grad_cells: float32 [8192, 256], P('cell')
- grad_descs: float32 [8192, 256], P('desc')
All inputs are finite; a program needn't handle non-finite values.
Results may differ from a plain program's by a relative error of at most 0.0003.
Values sent between devices are 32-bit elements; how exact they have to be, the bound alone decides.
A program may use at most 192 MiB of HBM per device.

v0:
```python
import math
import jax
import jax.numpy as jnp
from jax import lax
from jax.sharding import PartitionSpec as P

ITERS = 4


def combined_all(value, axis, join):
    pieces = jax.tree.map(lambda part: lax.all_gather(part, axis), value)
    head = jax.tree.map(lambda part: part[0], pieces)
    tail = jax.tree.map(lambda part: part[1:], pieces)
    so_far, _ = lax.scan(lambda so_far, share: (join(so_far, share), None), head, tail)
    return so_far


def lse_merge(first, second):
    max_one, sum_one = first
    max_two, sum_two = second
    top = jnp.maximum(max_one, max_two)
    return (top, sum_one * jnp.exp(max_one - top) + sum_two * jnp.exp(max_two - top))


def plan_adjoint(xrows, ycols, g_first, cf_rows, cg_cols, over_rows, over_cols, sum_rows, sum_cols):
    scale = 2.0 / math.sqrt(xrows.shape[1])
    highest = lax.Precision.HIGHEST
    logit = (
        lax.dot_general(
            xrows,
            ycols,
            (((1,), (1,)), ((), ())),
            precision=highest,
            preferred_element_type=jnp.float32,
        )
        * scale
    )
    g_now = g_first
    f_list = []
    g_list = [g_first]
    for step in range(ITERS):
        zvals = logit + g_now[None, :]
        row_max = jnp.max(zvals, axis=1)
        row_sum = jnp.sum(jnp.exp(zvals - row_max[:, None]), axis=1)
        row_max, row_sum = over_rows(row_max, row_sum)
        f_now = -(row_max + jnp.log(row_sum))
        wvals = logit + f_now[:, None]
        col_max = jnp.max(wvals, axis=0)
        col_sum = jnp.sum(jnp.exp(wvals - col_max[None, :]), axis=0)
        col_max, col_sum = over_cols(col_max, col_sum)
        g_now = -(col_max + jnp.log(col_sum))
        f_list.append(f_now)
        g_list.append(g_now)
    gbar = cg_cols
    lbar = jnp.zeros_like(logit)
    for step in reversed(range(ITERS)):
        g_here = g_list[step + 1]
        bplan = jnp.exp(logit + f_list[step][:, None] + g_here[None, :])
        fbar = -sum_rows(jnp.sum(bplan * gbar[None, :], axis=1))
        if step == ITERS - 1:
            fbar = fbar + cf_rows
        aplan = bplan * jnp.exp(g_list[step] - g_here)[None, :]
        lbar = lbar - (bplan * gbar[None, :] + aplan * fbar[:, None])
        if step > 0:
            gbar = -sum_cols(jnp.sum(aplan * fbar[:, None], axis=0))
    return (lbar, scale)


def on_device(cells, descs, g_start, cot_f, cot_g):
    highest = lax.Precision.HIGHEST
    lbar, scale = plan_adjoint(
        cells,
        descs,
        g_start,
        cot_f,
        cot_g,
        lambda big, total: combined_all((big, total), "desc", lse_merge),
        lambda big, total: combined_all((big, total), "cell", lse_merge),
        lambda part: lax.psum(part, "desc"),
        lambda part: lax.psum(part, "cell"),
    )
    part_x = scale * jnp.dot(lbar, descs, precision=highest, preferred_element_type=jnp.float32)
    part_y = scale * lax.dot_general(
        lbar, cells, (((0,), (0,)), ((), ())), precision=highest, preferred_element_type=jnp.float32
    )
    grad_cells = lax.psum(part_x, "desc")
    grad_descs = lax.psum(part_y, "cell")
    return (grad_cells, grad_descs)


def solution(mesh):
    placed = (P("cell", None), P("desc", None), P("desc"), P("cell"), P("desc"))
    return jax.shard_map(
        on_device,
        mesh=mesh,
        in_specs=placed,
        out_specs=(P("cell", None), P("desc", None)),
        check_vma=False,
    )
```

profile of v0, /device:TPU:0, one launch (start us, length us, event | category | flops | bytes accessed | tf_op | source)
XLA Modules:
  0.0 670.6 jit_solution(9534914086355051639)
XLA Ops:
  7.2 1.5 copy-done
  8.8 9.0 %add_reduce_fusion.3 = (f32[1024]{0:T(1024)S(1)}, f32[1024,2048]{1,0:T(8,128)S(1)}) fusion(f32[2048]{0:T(1024)} %param.23, f32[1024,256]{1,0:T(8,128)} %param.21, f32[2048,256]{1,0:T(8,128)S(1)} %copy-done), kind=kOutput, calls=%fused_computation.47 | convolution fusion | flops 6448741376 | bytes 11546624 | tf_op jit(solution)/shard_map/dot_general | solution.py:29
  17.8 6.3 all-gather
  24.1 2.0 exponential_reduce_fusion.7
  26.1 5.4 all-gather.1
  31.5 0.2 while.96
  31.7 4.2 add_reduce_fusion.7
  35.9 1.6 copy-done.2
  37.5 1.8 exponential_reduce_fusion.6
  39.3 31.1 %all-gather.2 = f32[16384]{0:T(1024)S(1)} all-gather(f32[2048]{0:T(1024)S(1)} %add_reduce_fusion.7), channel_id=4, replica_groups=mesh['cell'=8,'desc'=4] {'cell'}, dimensions={0}, use_global_device_ids=true | all-gather | bytes 73728 | tf_op jit(solution)/shard_map/all_gather | solution.py:11
  70.3 30.7 %all-gather.3 = f32[16384]{0:T(1024)S(1)} all-gather(f32[2048]{0:T(1024)S(1)} %exponential_reduce_fusion.6), channel_id=5, replica_groups=mesh['cell'=8,'desc'=4] {'cell'}, dimensions={0}, use_global_device_ids=true | all-gather | bytes 73728 | tf_op jit(solution)/shard_map/all_gather | solution.py:11
  101.1 0.4 while.97
  101.6 4.0 add_reduce_fusion.2
  105.6 4.4 exponential_reduce_fusion.5
  109.9 5.2 all-gather.4
  115.1 5.2 all-gather.5
  120.4 0.2 while.98
  120.5 4.0 add_reduce_fusion.6
  124.5 4.3 exponential_reduce_fusion.4
  128.9 30.5 %all-gather.6 = f32[16384]{0:T(1024)S(1)} all-gather(f32[2048]{0:T(1024)S(1)} %add_reduce_fusion.6), channel_id=8, replica_groups=mesh['cell'=8,'desc'=4] {'cell'}, dimensions={0}, use_global_device_ids=true | all-gather | bytes 73728 | tf_op jit(solution)/shard_map/all_gather | solution.py:11
  159.4 30.5 %all-gather.7 = f32[16384]{0:T(1024)S(1)} all-gather(f32[2048]{0:T(1024)S(1)} %exponential_reduce_fusion.4), channel_id=9, replica_groups=mesh['cell'=8,'desc'=4] {'cell'}, dimensions={0}, use_global_device_ids=true | all-gather | bytes 73728 | tf_op jit(solution)/shard_map/all_gather | solution.py:11
  190.0 0.4 while.99
  190.5 4.0 add_reduce_fusion.1
  194.5 4.4 exponential_reduce_fusion.3
  198.8 5.2 all-gather.8
  204.0 5.2 all-gather.9
  209.4 4.0 add_reduce_fusion.5
  213.4 4.3 exponential_reduce_fusion.2
  217.8 30.5 %all-gather.10 = f32[16384]{0:T(1024)S(1)} all-gather(f32[2048]{0:T(1024)S(1)} %add_reduce_fusion.5), channel_id=12, replica_groups=mesh['cell'=8,'desc'=4] {'cell'}, dimensions={0}, use_global_device_ids=true | all-gather | bytes 73728 | tf_op jit(solution)/shard_map/all_gather | solution.py:11
  248.3 30.5 %all-gather.11 = f32[16384]{0:T(1024)S(1)} all-gather(f32[2048]{0:T(1024)S(1)} %exponential_reduce_fusion.2), channel_id=13, replica_groups=mesh['cell'=8,'desc'=4] {'cell'}, dimensions={0}, use_global_device_ids=true | all-gather | bytes 73728 | tf_op jit(solution)/shard_map/all_gather | solution.py:11
  278.9 0.4 while.101
  279.3 4.0 add_reduce_fusion
  283.4 4.4 exponential_reduce_fusion.1
  287.8 5.2 all-gather.12
  293.0 5.4 all-gather.13
  298.4 0.2 while.102
  298.6 4.0 add_reduce_fusion.4
  302.6 4.3 exponential_reduce_fusion
  306.9 30.5 %all-gather.14 = f32[16384]{0:T(1024)S(1)} all-gather(f32[2048]{0:T(1024)S(1)} %add_reduce_fusion.4), channel_id=16, replica_groups=mesh['cell'=8,'desc'=4] {'cell'}, dimensions={0}, use_global_device_ids=true | all-gather | bytes 73728 | tf_op jit(solution)/shard_map/all_gather | solution.py:11
  337.5 30.5 %all-gather.15 = f32[16384]{0:T(1024)S(1)} all-gather(f32[2048]{0:T(1024)S(1)} %exponential_reduce_fusion), channel_id=17, replica_groups=mesh['cell'=8,'desc'=4] {'cell'}, dimensions={0}, use_global_device_ids=true | all-gather | bytes 73728 | tf_op jit(solution)/shard_map/all_gather | solution.py:11
  368.1 0.4 while.103
  368.5 4.5 multiply_reduce_fusion.3
  373.1 5.7 psum.63
  378.7 4.7 fusion
  383.4 21.5 %psum.64 = f32[2048]{0:T(1024)S(1)} all-reduce(f32[2048]{0:T(1024)S(1)} %fusion), channel_id=1, replica_groups=mesh['cell'=8,'desc'=4] {'cell'}, use_global_device_ids=true, to_apply=%region_35.36 | all-reduce | flops 2048 | bytes 16384 | tf_op jit(solution)/shard_map/psum | solution.py:80
  404.9 4.5 multiply_reduce_fusion.2
  409.4 5.7 psum.65
  415.1 4.6 fusion.1
  419.7 17.4 %psum.66 = f32[2048]{0:T(1024)S(1)} all-reduce(f32[2048]{0:T(1024)S(1)} %fusion.1), channel_id=1, replica_groups=mesh['cell'=8,'desc'=4] {'cell'}, use_global_device_ids=true, to_apply=%region_39.40 | all-reduce | flops 2048 | bytes 16384 | tf_op jit(solution)/shard_map/psum | solution.py:80
  437.1 4.5 multiply_reduce_fusion.1
  441.7 5.7 psum.67
  447.3 4.6 fusion.2
  452.0 19.4 %psum.68 = f32[2048]{0:T(1024)S(1)} all-reduce(f32[2048]{0:T(1024)S(1)} %fusion.2), channel_id=1, replica_groups=mesh['cell'=8,'desc'=4] {'cell'}, use_global_device_ids=true, to_apply=%region_43.44 | all-reduce | flops 2048 | bytes 16384 | tf_op jit(solution)/shard_map/psum | solution.py:80
  471.4 4.5 multiply_reduce_fusion
  475.9 6.1 psum.69
  482.0 24.1 %add_subtract_fusion = f32[1024,2048]{1,0:T(8,128)S(1)} fusion(f32[1024,2048]{1,0:T(8,128)} %copy-done.1, f32[1024]{0:T(1024)S(1)} %neg.59, f32[2048]{0:T(1024)S(1)} %get-tuple-element.338, f32[2048]{0:T(1024)S(1)} %neg.58, f32[1024]{0:T(1024)S(1)} %neg.57, f32[2048]{0:T(1024)S(1)} %get-tuple-element.340, f32[2048]{0:T(1024)S(1)} %neg.56, f32[1024]{0:T(1024)S(1)} %neg.55, ...), kind=kLoop, calls=%fused_computation.24 | loop fusion | flops 58720256 | bytes 16908288 | tf_op jit(solution)/shard_map/sub | solution.py:63
  506.1 3.2 copy-done.3
  509.3 7.6 %convolution_multiply_fusion.2 = f32[1024,256]{1,0:T(8,128)} fusion(f32[1024,2048]{1,0:T(8,128)S(1)} %add_subtract_fusion, f32[2048,256]{1,0:T(8,128)S(1)} %copy-done), kind=kOutput, calls=%fused_computation.57 | convolution fusion | flops 6442713088 | bytes 11534336 | tf_op jit(solution)/shard_map/dot_general | solution.py:82
  516.9 0.2 all-reduce.5.cloned.1.call-start
  517.2 16.5 %convolution_multiply_fusion.1 = f32[2048,256]{1,0:T(8,128)} fusion(f32[1024,2048]{1,0:T(8,128)} %copy-done.3, f32[1024,256]{1,0:T(8,128)S(1)} %copy-done.4), kind=kOutput, calls=%fused_computation.56 | convolution fusion | flops 6442975232 | bytes 11534336 | tf_op jit(solution)/shard_map/dot_general | solution.py:83
  533.7 17.5 %all-reduce.3.cloned.1.call-done = f32[1024,256]{1,0:T(8,128)} async-done(((f32[1024,256]{1,0:T(8,128)}), f32[1024,256]{1,0:T(8,128)}) %all-reduce.3.cloned.1.call-update) | async-done | bytes 1048592 | tf_op jit(solution)/shard_map/psum | solution.py:86
  551.3 107.0 %all-reduce.5.cloned.1.call-done = f32[2048,256]{1,0:T(8,128)} async-done(((f32[2048,256]{1,0:T(8,128)}), f32[2048,256]{1,0:T(8,128)}) %all-reduce.5.cloned.1.call-update) | async-done | bytes 2097168 | tf_op jit(solution)/shard_map/psum | solution.py:87
  658.2 2.3 copy.83
  660.5 3.0 copy.84
  (160 shorter events, 1.8 us)
Async XLA Ops:
  7.2 1.6 copy-start
  7.2 16.9 %copy-start.5 = (f32[2048]{0:T(1024)S(1)}, f32[2048]{0:T(1024)}, u32[]{:S(2)}) copy-start(f32[2048]{0:T(1024)} %param.23) | copy-start | bytes 24580
  7.2 544.1 %all-reduce.3.cloned.1.call-start = ((), (), s32[]{:S(2)}) async-start(), calls=%async_computation | async-start | bytes 2097152 | tf_op jit(solution)/shard_map/psum | solution.py:86
  17.8 6.3 copy-start.1
  31.7 5.8 copy-start.2
  298.6 69.9 %copy-start.6 = (f32[2048]{0:T(1024)S(1)}, f32[2048]{0:T(1024)}, u32[]{:S(2)}) copy-start(f32[2048]{0:T(1024)} %param.25) | copy-start | bytes 24580
  302.6 76.1 %copy-start.7 = (f32[1024]{0:T(1024)S(1)}, f32[1024]{0:T(1024)}, u32[]{:S(2)}) copy-start(f32[1024]{0:T(1024)} %param.24) | copy-start | bytes 12292
  506.1 3.2 copy-start.3
  509.3 7.9 %copy-start.4 = (f32[1024,256]{1,0:T(8,128)S(1)}, f32[1024,256]{1,0:T(8,128)}, u32[]{:S(2)}) copy-start(f32[1024,256]{1,0:T(8,128)} %param.21) | copy-start | bytes 3145732
  516.9 141.3 %all-reduce.5.cloned.1.call-start = ((), (), s32[]{:S(2)}) async-start(), calls=%async_computation.1 | async-start | bytes 4194304 | tf_op jit(solution)/shard_map/psum | solution.py:87
Sparse Core Ops, SparseCore 0:
  517.1 34.1 all-reduce.2
  555.5 102.7 all-reduce.4
where the time goes:
time: 679 us; the launch traced here: 671 us
  blocking collectives  369 us (54%)
  waiting for transfers between devices  125 us (18%)
  other arithmetic  115 us (17%)
  matrix products  33.2 us (5%)
  between operations  14.7 us (2%)
  local copies, waits for them, and re-layouts  12.6 us (2%)
    all_gather x16, blocking collectives, combined_all(): pieces = jax.tree.map(lambda part: lax.all_gather(part, axis), value)  288 us
    psum x1, waiting for transfers between devices, on_device(): grad_descs = lax.psum(part_y, 'cell')  107 us
    psum x3, blocking collectives, on_device(): lax.psum(part, 'cell')  58.3 us
    sub x1, other arithmetic, plan_adjoint(): lbar = lbar - (bplan * gbar[None, :] + aplan * fbar[:, None])  24.1 us
    psum x4, blocking collectives, on_device(): lax.psum(part, 'desc')  23.1 us
    reduce_sum x4, other arithmetic, plan_adjoint(): fbar = -sum_rows(jnp.sum(bplan * gbar[None, :], axis=1))  18.1 us
    psum x1, waiting for transfers between devices, on_device(): grad_cells = lax.psum(part_x, 'desc')  17.5 us
    dot_general x1, matrix products, on_device(): lax.dot_general(lbar, cells, (((0,), (0,)), ((), ())), precision=highest,...  16.5 us
  transfers between devices with their start and end apart: 2, of which 2 were waited for; matrix products, arithmetic and copies ran while one was open for 2% of the time, Pallas kernels for 0%

commit v1 on v0

--- a/solution.py
+++ b/solution.py
@@ -5,6 +5,14 @@
 from jax.sharding import PartitionSpec as P
 
 ITERS = 4
+
+
+def add_in_pairs(x, axis):
+    size, acc = (lax.axis_size(axis), x)
+    for far in [1 << k for k in range(size.bit_length() - 1)]:
+        swap = [(i, i ^ far) for i in range(size)]
+        acc = acc + lax.ppermute(acc, axis, swap)
+    return acc
 
 
 def combined_all(value, axis, join):
@@ -84,7 +92,7 @@
         lbar, cells, (((0,), (0,)), ((), ())), precision=highest, preferred_element_type=jnp.float32
     )
     grad_cells = lax.psum(part_x, "desc")
-    grad_descs = lax.psum(part_y, "cell")
+    grad_descs = add_in_pairs(part_y, "cell")
     return (grad_cells, grad_descs)
 
 

time: 679 us -> 730 us (1.075)
  waiting for transfers between devices: 125 us -> 179 us
    ppermute x0 -> x3, waiting for transfers between devices: none -> 179 us  [add_in_pairs(): acc = acc + lax.ppermute(acc, axis, swap)]
    psum x1 -> x0, waiting for transfers between devices: 107 us -> none  [on_device(): grad_descs = lax.psum(part_y, 'cell')]
    psum x1, waiting for transfers between devices: 17.5 us -> 0.01 us  [on_device(): grad_cells = lax.psum(part_x, 'desc')]
  transfers between devices with their start and end apart: 2 -> 4, of which waited for: 2 -> 3; matrix products, arithmetic and copies ran while one was open for 2% -> 2% of each run, Pallas kernels for 0% -> 0%
where the time goes in v1:
time: 730 us; the launch traced here: 722 us
  blocking collectives  369 us (51%)
  waiting for transfers between devices  179 us (25%)
  other arithmetic  121 us (17%)
  matrix products  30.1 us (4%)
  between operations  14.7 us (2%)
    all_gather x16, blocking collectives, combined_all(): pieces = jax.tree.map(lambda part: lax.all_gather(part, axis), value)  288 us
    ppermute x3, waiting for transfers between devices, add_in_pairs(): acc = acc + lax.ppermute(acc, axis, swap)  179 us
    psum x3, blocking collectives, on_device(): lax.psum(part, 'cell')  58.3 us
    sub x1, other arithmetic, plan_adjoint(): lbar = lbar - (bplan * gbar[None, :] + aplan * fbar[:, None])  24.6 us
    psum x4, blocking collectives, on_device(): lax.psum(part, 'desc')  22.7 us
    reduce_sum x4, other arithmetic, plan_adjoint(): fbar = -sum_rows(jnp.sum(bplan * gbar[None, :], axis=1))  18.1 us
    reduce_max x4, other arithmetic, plan_adjoint(): col_max = jnp.max(wvals, axis=0)  16.2 us
    reduce_sum x4, other arithmetic, plan_adjoint(): row_sum = jnp.sum(jnp.exp(zvals - row_max[:, None]), axis=1)  15.1 us
  transfers between devices with their start and end apart: 4, of which 3 were waited for; matrix products, arithmetic and copies ran while one was open for 2% of the time, Pallas kernels for 0%

profile of v1, /device:TPU:0, one launch (start us, length us, event | category | flops | bytes accessed | tf_op | source)
XLA Modules:
  0.0 721.8 jit_solution(7140182591552215706)
XLA Ops:
  7.2 1.5 copy-done
  8.8 9.0 %add_reduce_fusion.3 = (f32[1024]{0:T(1024)S(1)}, f32[1024,2048]{1,0:T(8,128)S(1)}) fusion(f32[2048]{0:T(1024)} %param.23, f32[1024,256]{1,0:T(8,128)} %param.21, f32[2048,256]{1,0:T(8,128)S(1)} %copy-done), kind=kOutput, calls=%fused_computation.47 | convolution fusion | flops 6448741376 | bytes 11546624 | tf_op jit(solution)/shard_map/dot_general | solution.py:37
  17.8 6.3 all-gather
  24.1 2.0 exponential_reduce_fusion.7
  26.1 5.4 all-gather.1
  31.5 0.2 while.96
  31.7 4.2 add_reduce_fusion.7
  35.9 1.6 copy-done.2
  37.5 1.8 exponential_reduce_fusion.6
  39.3 31.1 %all-gather.2 = f32[16384]{0:T(1024)S(1)} all-gather(f32[2048]{0:T(1024)S(1)} %add_reduce_fusion.7), channel_id=4, replica_groups=mesh['cell'=8,'desc'=4] {'cell'}, dimensions={0}, use_global_device_ids=true | all-gather | bytes 73728 | tf_op jit(solution)/shard_map/all_gather | solution.py:19
  70.3 31.0 %all-gather.3 = f32[16384]{0:T(1024)S(1)} all-gather(f32[2048]{0:T(1024)S(1)} %exponential_reduce_fusion.6), channel_id=5, replica_groups=mesh['cell'=8,'desc'=4] {'cell'}, dimensions={0}, use_global_device_ids=true | all-gather | bytes 73728 | tf_op jit(solution)/shard_map/all_gather | solution.py:19
  101.4 0.4 while.97
  101.8 4.0 add_reduce_fusion.2
  105.9 4.4 exponential_reduce_fusion.5
  110.2 5.2 all-gather.4
  115.4 5.2 all-gather.5
  120.6 0.2 while.98
  120.8 4.0 add_reduce_fusion.6
  124.8 4.3 exponential_reduce_fusion.4
  129.2 30.5 %all-gather.6 = f32[16384]{0:T(1024)S(1)} all-gather(f32[2048]{0:T(1024)S(1)} %add_reduce_fusion.6), channel_id=8, replica_groups=mesh['cell'=8,'desc'=4] {'cell'}, dimensions={0}, use_global_device_ids=true | all-gather | bytes 73728 | tf_op jit(solution)/shard_map/all_gather | solution.py:19
  159.7 30.5 %all-gather.7 = f32[16384]{0:T(1024)S(1)} all-gather(f32[2048]{0:T(1024)S(1)} %exponential_reduce_fusion.4), channel_id=9, replica_groups=mesh['cell'=8,'desc'=4] {'cell'}, dimensions={0}, use_global_device_ids=true | all-gather | bytes 73728 | tf_op jit(solution)/shard_map/all_gather | solution.py:19
  190.3 0.4 while.99
  190.7 4.0 add_reduce_fusion.1
  194.8 4.4 exponential_reduce_fusion.3
  199.1 5.2 all-gather.8
  204.3 5.2 all-gather.9
  209.7 4.0 add_reduce_fusion.5
  213.7 4.3 exponential_reduce_fusion.2
  218.0 30.5 %all-gather.10 = f32[16384]{0:T(1024)S(1)} all-gather(f32[2048]{0:T(1024)S(1)} %add_reduce_fusion.5), channel_id=12, replica_groups=mesh['cell'=8,'desc'=4] {'cell'}, dimensions={0}, use_global_device_ids=true | all-gather | bytes 73728 | tf_op jit(solution)/shard_map/all_gather | solution.py:19
  248.6 30.5 %all-gather.11 = f32[16384]{0:T(1024)S(1)} all-gather(f32[2048]{0:T(1024)S(1)} %exponential_reduce_fusion.2), channel_id=13, replica_groups=mesh['cell'=8,'desc'=4] {'cell'}, dimensions={0}, use_global_device_ids=true | all-gather | bytes 73728 | tf_op jit(solution)/shard_map/all_gather | solution.py:19
  279.2 0.4 while.101
  279.6 4.0 add_reduce_fusion
  283.7 4.4 exponential_reduce_fusion.1
  288.0 5.2 all-gather.12
  293.3 5.4 all-gather.13
  298.8 4.0 add_reduce_fusion.4
  302.9 4.3 exponential_reduce_fusion
  307.2 30.5 %all-gather.14 = f32[16384]{0:T(1024)S(1)} all-gather(f32[2048]{0:T(1024)S(1)} %add_reduce_fusion.4), channel_id=16, replica_groups=mesh['cell'=8,'desc'=4] {'cell'}, dimensions={0}, use_global_device_ids=true | all-gather | bytes 73728 | tf_op jit(solution)/shard_map/all_gather | solution.py:19
  337.7 30.5 %all-gather.15 = f32[16384]{0:T(1024)S(1)} all-gather(f32[2048]{0:T(1024)S(1)} %exponential_reduce_fusion), channel_id=17, replica_groups=mesh['cell'=8,'desc'=4] {'cell'}, dimensions={0}, use_global_device_ids=true | all-gather | bytes 73728 | tf_op jit(solution)/shard_map/all_gather | solution.py:19
  368.3 0.4 while.103
  368.8 4.5 multiply_reduce_fusion.3
  373.3 5.7 psum.56
  379.0 4.7 fusion
  383.7 21.5 %psum.57 = f32[2048]{0:T(1024)S(1)} all-reduce(f32[2048]{0:T(1024)S(1)} %fusion), channel_id=1, replica_groups=mesh['cell'=8,'desc'=4] {'cell'}, use_global_device_ids=true, to_apply=%region_35.36 | all-reduce | flops 2048 | bytes 16384 | tf_op jit(solution)/shard_map/psum | solution.py:88
  405.2 4.5 multiply_reduce_fusion.2
  409.7 5.7 psum.58
  415.4 4.6 fusion.1
  420.0 17.4 %psum.59 = f32[2048]{0:T(1024)S(1)} all-reduce(f32[2048]{0:T(1024)S(1)} %fusion.1), channel_id=1, replica_groups=mesh['cell'=8,'desc'=4] {'cell'}, use_global_device_ids=true, to_apply=%region_39.40 | all-reduce | flops 2048 | bytes 16384 | tf_op jit(solution)/shard_map/psum | solution.py:88
  437.4 4.5 multiply_reduce_fusion.1
  441.9 5.7 psum.60
  447.6 4.6 fusion.2
  452.3 19.4 %psum.61 = f32[2048]{0:T(1024)S(1)} all-reduce(f32[2048]{0:T(1024)S(1)} %fusion.2), channel_id=1, replica_groups=mesh['cell'=8,'desc'=4] {'cell'}, use_global_device_ids=true, to_apply=%region_43.44 | all-reduce | flops 2048 | bytes 16384 | tf_op jit(solution)/shard_map/psum | solution.py:88
  471.7 4.5 multiply_reduce_fusion
  476.2 5.7 psum.62
  481.8 24.6 %add_subtract_fusion = f32[1024,2048]{1,0:T(8,128)S(1)} fusion(f32[1024,2048]{1,0:T(8,128)} %copy-done.1, f32[1024]{0:T(1024)S(1)} %neg.59, f32[2048]{0:T(1024)S(1)} %get-tuple-element.338, f32[2048]{0:T(1024)S(1)} %neg.58, f32[1024]{0:T(1024)S(1)} %neg.57, f32[2048]{0:T(1024)S(1)} %get-tuple-element.340, f32[2048]{0:T(1024)S(1)} %neg.56, f32[1024]{0:T(1024)S(1)} %neg.55, ...), kind=kLoop, calls=%fused_computation.24 | loop fusion | flops 58720256 | bytes 16908288 | tf_op jit(solution)/shard_map/sub | solution.py:71
  506.4 13.4 %convolution_multiply_fusion.1 = f32[2048,256]{1,0:T(8,128)S(1)} fusion(f32[1024,2048]{1,0:T(8,128)S(1)} %add_subtract_fusion, f32[1024,256]{1,0:T(8,128)S(1)} %copy-done.3), kind=kOutput, calls=%fused_computation.56 | convolution fusion | flops 6442975232 | bytes 11534336 | tf_op jit(solution)/shard_map/dot_general | solution.py:91
  519.9 47.7 %collective-permute-done = f32[2048,256]{1,0:T(8,128)S(1)} collective-permute-done((f32[2048,256]{1,0:T(8,128)S(1)}, f32[2048,256]{1,0:T(8,128)S(1)}, u32[]{:S(2)}, u32[]{:S(2)}) %collective-permute-start) | collective-permute-done | bytes 2097184 | tf_op jit(solution)/shard_map/ppermute | solution.py:14
  567.7 0.3 add.252
  568.0 46.9 %collective-permute-done.1 = f32[2048,256]{1,0:T(8,128)S(1)} collective-permute-done((f32[2048,256]{1,0:T(8,128)S(1)}, f32[2048,256]{1,0:T(8,128)S(1)}, u32[]{:S(2)}, u32[]{:S(2)}) %collective-permute-start.1) | collective-permute-done | bytes 2097184 | tf_op jit(solution)/shard_map/ppermute | solution.py:14
  614.9 1.6 add.253
  616.5 7.6 %convolution_multiply_fusion.2 = f32[1024,256]{1,0:T(8,128)} fusion(f32[1024,2048]{1,0:T(8,128)S(1)} %add_subtract_fusion, f32[2048,256]{1,0:T(8,128)S(1)} %copy-done), kind=kOutput, calls=%fused_computation.57 | convolution fusion | flops 6442713088 | bytes 11534336 | tf_op jit(solution)/shard_map/dot_general | solution.py:90
  624.2 84.5 %collective-permute-done.2 = f32[2048,256]{1,0:T(8,128)} collective-permute-done((f32[2048,256]{1,0:T(8,128)}, f32[2048,256]{1,0:T(8,128)}, u32[]{:S(2)}, u32[]{:S(2)}) %collective-permute-start.2) | collective-permute-done | bytes 2097184 | tf_op jit(solution)/shard_map/ppermute | solution.py:14
  708.7 3.8 add.254
  712.5 2.3 copy.82
  (163 shorter events, 2.1 us)
Async XLA Ops:
  7.2 1.6 copy-start
  7.2 16.9 %copy-start.4 = (f32[2048]{0:T(1024)S(1)}, f32[2048]{0:T(1024)}, u32[]{:S(2)}) copy-start(f32[2048]{0:T(1024)} %param.23) | copy-start | bytes 24580
  7.2 705.3 %all-reduce.2.cloned.1.call-start = ((), (), s32[]{:S(2)}) async-start(), calls=%async_computation | async-start | bytes 2097152 | tf_op jit(solution)/shard_map/psum | solution.py:94
  17.8 6.3 copy-start.1
  31.7 5.8 copy-start.2
  298.8 69.9 %copy-start.5 = (f32[2048]{0:T(1024)S(1)}, f32[2048]{0:T(1024)}, u32[]{:S(2)}) copy-start(f32[2048]{0:T(1024)} %param.25) | copy-start | bytes 24580
  302.9 76.1 %copy-start.6 = (f32[1024]{0:T(1024)S(1)}, f32[1024]{0:T(1024)}, u32[]{:S(2)}) copy-start(f32[1024]{0:T(1024)} %param.24) | copy-start | bytes 12292
  481.8 24.6 %copy-start.3 = (f32[1024,256]{1,0:T(8,128)S(1)}, f32[1024,256]{1,0:T(8,128)}, u32[]{:S(2)}) copy-start(f32[1024,256]{1,0:T(8,128)} %param.21) | copy-start | bytes 3145732
  519.9 47.8 %collective-permute-start = (f32[2048,256]{1,0:T(8,128)S(1)}, f32[2048,256]{1,0:T(8,128)S(1)}, u32[]{:S(2)}, u32[]{:S(2)}) collective-permute-start(f32[2048,256]{1,0:T(8,128)S(1)} %convolution_multiply_fusion.1), channel_id=1, source_target_pairs={{0,4},{4,0},{8,12},{12,8},{16,20},{20,16},{24,28},{28,24},{1,5},{5... | collective-permute-start | bytes 6291464 | tf_op jit(solution)/shard_map/ppermute | solution.py:14
  568.0 47.0 %collective-permute-start.1 = (f32[2048,256]{1,0:T(8,128)S(1)}, f32[2048,256]{1,0:T(8,128)S(1)}, u32[]{:S(2)}, u32[]{:S(2)}) collective-permute-start(f32[2048,256]{1,0:T(8,128)S(1)} %add.252), channel_id=1, source_target_pairs={{0,8},{4,12},{8,0},{12,4},{16,24},{20,28},{24,16},{28,20},{1,9},{5... | collective-permute-start | bytes 6291464 | tf_op jit(solution)/shard_map/ppermute | solution.py:14
  616.5 92.2 %collective-permute-start.2 = (f32[2048,256]{1,0:T(8,128)}, f32[2048,256]{1,0:T(8,128)}, u32[]{:S(2)}, u32[]{:S(2)}) collective-permute-start(f32[2048,256]{1,0:T(8,128)} %add.253), channel_id=1, source_target_pairs={{0,16},{4,20},{8,24},{12,28},{16,0},{20,4},{24,8},{28,12},{1,17},{... | collective-permute-start | bytes 6291464 | tf_op jit(solution)/shard_map/ppermute | solution.py:14
Sparse Core Ops, SparseCore 0:
  624.3 35.5 all-reduce.1
